TPU v7x, 1024 devices: a whole 4x4x32 slice. The times are simulated.
1024 devices in a mesh: space: 64 (over x, z_hi, y, core), chan: 16 (over z_lo).
Axes of the slice: x: 4, y: 4, z: 32 (z_hi: 2, z_lo: 16; z = z_hi * 16 + z_lo), core: 2. Of those that a mesh axis runs over, the one named last changes fastest.
Arguments:
- volume: bfloat16 [32, 128, 32, 128], P(None, 'space', 'chan'), may hold values from -6 to 6
- weight_first: bfloat16 [3, 3, 3, 64, 32], replicated, may hold values from -0.21875 to 0.21875
- weight_deep: bfloat16 [3, 3, 3, 512, 64], P(None, None, None, 'chan'), may hold values from -0.15625 to 0.15625
- cotangent: bfloat16 [512, 64, 1024], P('chan', 'space'), may hold values from -6 to 6
Outputs:
- deep_out: bfloat16 [512, 64, 1024], P('chan', 'space')
- grad_deep: float32 [3, 3, 3, 512, 64], P(None, None, None, 'chan')
All inputs are finite; a program needn't handle non-finite values.
Results may differ from a plain program's by a relative error of at most 0.0051.
Values may be sent and summed in bfloat16 or wider, within the bound.
A program may use at most 32 MiB of HBM per device.

v0:
```python
import jax
import jax.numpy as jnp
from jax import lax
from jax.sharding import PartitionSpec as P


def padded_2(array, sides, width):
    for axis, dim in sides:
        peers, length = (lax.axis_size(axis), array.shape[dim])
        up = [(i, (i + 1) % peers) for i in range(peers - 1)]
        down = [(j, i) for i, j in up]
        last = lax.slice_in_dim(array, length - width, length, axis=dim)
        leading = lax.slice_in_dim(array, 0, width, axis=dim)
        before = lax.ppermute(last, axis, up)
        after = lax.ppermute(leading, axis, down)
        array = jnp.concatenate([before, array, after], axis=dim)
    return array


def convolve(padded, weight, planes, rows, depth):
    total = jnp.zeros((weight.shape[3], planes, rows, depth), jnp.float32)
    for offset_x in range(3):
        for offset_y in range(3):
            for offset_z in range(3):
                window = padded[
                    :,
                    offset_x : offset_x + planes,
                    offset_y : offset_y + rows,
                    offset_z : offset_z + depth,
                ]
                total = total + jnp.einsum(
                    "oc,cxyz->oxyz",
                    weight[offset_x, offset_y, offset_z],
                    window,
                    preferred_element_type=jnp.float32,
                )
    return total


def weight_terms(grad_pre, padded, planes, rows, depth):
    outer = []
    for offset_x in range(3):
        middle = []
        for offset_y in range(3):
            inner = []
            for offset_z in range(3):
                window = padded[
                    :,
                    offset_x : offset_x + planes,
                    offset_y : offset_y + rows,
                    offset_z : offset_z + depth,
                ]
                inner.append(
                    jnp.einsum(
                        "oxyz,cxyz->oc", grad_pre, window, preferred_element_type=jnp.float32
                    )
                )
            middle.append(jnp.stack(inner))
        outer.append(jnp.stack(middle))
    return jnp.stack(outer)


def pool_mean(act):
    chans, planes, rows, depth = act.shape
    blocks = act.reshape(chans, planes // 2, 2, rows // 2, 2, depth // 2, 2)
    return jnp.mean(blocks, axis=(2, 4, 6))


def on_device(volume, weight_first, weight_deep, cotangent):
    planes = volume.shape[1]
    rows = volume.shape[2]
    depth = volume.shape[3]
    rimmed = padded_2(volume, (("space", 1), ("chan", 2)), 1)
    padded = jnp.pad(rimmed, ((0, 0), (0, 0), (0, 0), (1, 1)))
    pre_first = convolve(padded, weight_first, planes, rows, depth)
    pooled = pool_mean(jax.nn.silu(pre_first)).astype(jnp.bfloat16)
    whole = lax.all_gather(pooled, "chan", axis=2, tiled=True)
    framed = padded_2(whole, (("space", 1),), 1)
    deep_in = jnp.pad(framed, ((0, 0), (0, 0), (1, 1), (1, 1)))
    deep_planes = pooled.shape[1]
    deep_rows = framed.shape[2]
    deep_depth = framed.shape[3]
    pre_deep = convolve(deep_in, weight_deep, deep_planes, deep_rows, deep_depth)
    out_chans = pre_deep.shape[0]
    deep_out = (
        jax.nn.silu(pre_deep)
        .astype(jnp.bfloat16)
        .reshape(out_chans, deep_planes, deep_rows * deep_depth)
    )
    sigma = jax.nn.sigmoid(pre_deep)
    cot_grid = cotangent.reshape(out_chans, deep_planes, deep_rows, deep_depth).astype(jnp.float32)
    grad_pre = (cot_grid * sigma * (1.0 + pre_deep * (1.0 - sigma))).astype(jnp.bfloat16)
    local_grad = weight_terms(grad_pre, deep_in, deep_planes, deep_rows, deep_depth)
    grad_deep = lax.psum(local_grad, "space")
    return (deep_out, grad_deep)


def solution(mesh):
    return jax.shard_map(
        on_device,
        mesh=mesh,
        in_specs=(
            P(None, "space", "chan", None),
            P(),
            P(None, None, None, "chan", None),
            P("chan", "space", None),
        ),
        out_specs=(P("chan", "space", None), P(None, None, None, "chan", None)),
        check_vma=False,
    )
```

profile of v0, /device:TPU:1, one launch (start us, length us, event | category | flops | bytes accessed | tf_op | source)
XLA Modules:
  0.0 1867.6 jit_solution(6404313522274778535)
XLA Ops:
  7.2 0.8 copy.25
  8.0 4.6 collective-permute-start
  12.6 12.8 collective-permute-start.1
  25.4 1.0 fusion.124
  26.4 0.8 constant_dynamic-update-slice_fusion.1
  27.2 1.3 collective-permute-start.2
  28.5 1.3 collective-permute-start.3
  29.8 0.9 convolution_bitcast_fusion.11
  30.7 2.8 collective-permute-done.3
  38.9 0.3 multiply_reduce_fusion
  39.5 95.8 %all-gather = bf16[64,1024]{0,1:T(8,128)(2,1)S(1)} all-gather(bf16[64,64]{0,1:T(8,128)(2,1)S(1)} %multiply_convert_fusion.1), channel_id=2, replica_groups=mesh['space'=64,'chan'=16] {'chan'}, dimensions={1}, use_global_device_ids=true | all-gather | bytes 139264 | tf_op jit(solution)/shard_map/all_gather | solution.py:77
  135.5 11.1 collective-permute-start.4
  146.6 1.9 collective-permute-start.5
  148.6 1.2 collective-permute-done.4
  149.9 4.4 collective-permute-done.5
  154.3 0.4 select_maximum_fusion
  155.6 0.3 convolution_bitcast_fusion.3
  155.9 0.3 convolution_add_fusion.14
  156.2 0.3 convolution_add_fusion.13
  157.0 0.3 convolution_add_fusion.9
  157.2 0.3 convolution_add_fusion.8
  157.7 0.3 convolution_add_fusion.6
  158.0 0.3 convolution_add_fusion.5
  158.4 0.3 convolution_add_fusion.3
  158.8 0.3 convolution_add_fusion.2
  159.2 0.3 fusion.5
  159.5 0.3 fusion.14
  159.8 0.3 fusion.13
  160.9 0.4 fusion.50
  161.5 0.3 convolution_bitcast_fusion.44
  161.9 0.3 convolution_bitcast_fusion.48
  162.2 0.3 convolution_bitcast_fusion.47
  162.7 0.3 convolution_bitcast_fusion.42
  163.0 0.3 convolution_bitcast_fusion.41
  163.7 0.3 convolution_bitcast_fusion.35
  164.1 0.3 convolution_bitcast_fusion.39
  164.4 0.3 convolution_bitcast_fusion.38
  164.9 0.3 convolution_bitcast_fusion.33
  165.2 0.3 convolution_bitcast_fusion.32
  165.7 0.3 convolution_bitcast_fusion.26
  166.1 0.3 convolution_bitcast_fusion.30
  166.4 0.3 convolution_bitcast_fusion.29
  166.9 0.3 convolution_bitcast_fusion.24
  167.2 0.3 convolution_bitcast_fusion.23
  168.0 0.8 pad_maximum_fusion
  168.9 0.8 reshape.285
  169.7 1689.2 %all-reduce.4.cloned.1.call-done = f32[3,3,3,32,64]{4,3,2,1,0:T(8,128)} async-done(((f32[3,3,3,32,64]{4,3,2,1,0:T(8,128)}), f32[3,3,3,32,64]{4,3,2,1,0:T(8,128)}) %all-reduce.4.cloned.1.call-update) | async-done | bytes 221200 | tf_op jit(solution)/shard_map/psum | solution.py:94
  1858.9 1.8 copy.86
  (81 shorter events, 11.2 us)
Async XLA Ops:
  7.2 26.5 %copy-start = (bf16[3,3,3,64,32]{3,4,2,1,0:T(8,128)(2,1)S(1)}, bf16[3,3,3,64,32]{3,4,2,1,0:T(8,128)(2,1)}, u32[]{:S(2)}) copy-start(bf16[3,3,3,64,32]{3,4,2,1,0:T(8,128)(2,1)} %param.5) | copy-start | bytes 331780
  7.2 1851.7 %all-reduce.4.cloned.1.call-start = ((), (), s32[]{:S(2)}) async-start(), calls=%async_computation | async-start | bytes 884736 | tf_op jit(solution)/shard_map/psum | solution.py:94
  8.0 18.3 collective-permute-start
  12.6 14.5 collective-permute-start.1
  27.2 3.5 collective-permute-start.2
  28.5 5.0 collective-permute-start.3
  39.3 109.2 %copy-start.2 = (bf16[32,1,1024]{2,0,1:T(8,128)(2,1)S(1)}, bf16[32,1,1024]{2,0,1:T(8,128)(2,1)}, u32[]{:S(2)}) copy-start(bf16[32,1,1024]{2,0,1:T(8,128)(2,1)} %param.7) | copy-start | bytes 196612
  135.5 14.4 collective-permute-start.4
  146.6 7.7 collective-permute-start.5
  148.6 6.1 copy-start.1
Sparse Core Ops, SparseCore 0:
  169.0 1689.9 all-reduce.3
where the time goes:
time: 1870 us
  waiting for transfers between devices  1700 us (91%)
  blocking collectives  95.8 us (5%)
  starting transfers between devices  33 us (2%)
  matrix products  20.4 us (1%)
    psum x1, waiting for transfers between devices, on_device(): grad_deep = lax.psum(local_grad, 'space')  1690 us
    all_gather x1, blocking collectives, on_device(): whole = lax.all_gather(pooled, 'chan', axis=2, tiled=True)  95.8 us
  transfers between devices with their start and end apart: 7, of which 4 were waited for; matrix products, arithmetic and copies ran while one was open for 0% of the time, Pallas kernels for 0%

commit v1 on v0

--- a/solution.py
+++ b/solution.py
@@ -1,6 +1,8 @@
 import jax
 import jax.numpy as jnp
 from jax import lax
+from jax.experimental import pallas as pl
+from jax.experimental.pallas import tpu as pltpu
 from jax.sharding import PartitionSpec as P
 
 
@@ -64,6 +66,102 @@
     chans, planes, rows, depth = act.shape
     blocks = act.reshape(chans, planes // 2, 2, rows // 2, 2, depth // 2, 2)
     return jnp.mean(blocks, axis=(2, 4, 6))
+
+
+MESH = pl.DeviceIdType.MESH
+CHUNKS = 27
+PLANE = 32
+
+
+def place(index, high):
+    return (index // 8) * 16 + high * 8 + index % 8
+
+
+def reduce_kernel(terms, total, parts, mine, far, sums, sems):
+    space = lax.axis_index("space")
+    high = (space // 8) % 2
+    here = (space // 16) * 8 + space % 8
+    other = place(here, 1 - high)
+    barrier = pltpu.get_barrier_semaphore()
+
+    def peer(step):
+        return (here + step) % PLANE
+
+    for step in range(1, PLANE):
+        pl.semaphore_signal(
+            barrier, inc=1, device_id={"space": place(peer(step), high)}, device_id_type=MESH
+        )
+    pl.semaphore_signal(barrier, inc=1, device_id={"space": other}, device_id_type=MESH)
+    pl.semaphore_wait(barrier, PLANE)
+    owner = here < CHUNKS
+
+    for step in range(1, PLANE):
+        to = peer(step)
+
+        @pl.when(to < CHUNKS)
+        def _():
+            pltpu.make_async_remote_copy(
+                terms.at[to],
+                parts.at[here],
+                sems.at[0],
+                sems.at[1],
+                device_id={"space": place(to, high)},
+                device_id_type=MESH,
+            ).start()
+
+    def sized(ref, sem):
+        return pltpu.make_async_copy(ref, ref, sem)
+
+    @pl.when(owner)
+    def _():
+        parts[here] = terms[here]
+        sized(parts.at[pl.ds(0, PLANE - 1)], sems.at[1]).wait()
+        mine[...] = jnp.sum(parts[...], axis=0)
+        swap = pltpu.make_async_remote_copy(
+            mine, far, sems.at[2], sems.at[3], device_id={"space": other}, device_id_type=MESH
+        )
+        swap.start()
+        swap.wait()
+        sums[here] = mine[...] + far[...]
+        for step in range(1, PLANE):
+            pltpu.make_async_remote_copy(
+                sums.at[here],
+                sums.at[here],
+                sems.at[4],
+                sems.at[5],
+                device_id={"space": place(peer(step), high)},
+                device_id_type=MESH,
+            ).start()
+        sized(sums.at[pl.ds(0, CHUNKS - 1)], sems.at[5]).wait()
+        sized(parts.at[pl.ds(0, PLANE - 1)], sems.at[4]).wait()
+        sized(terms.at[pl.ds(0, CHUNKS - 1)], sems.at[0]).wait()
+
+    @pl.when(jnp.logical_not(owner))
+    def _():
+        sized(sums, sems.at[5]).wait()
+        sized(terms, sems.at[0]).wait()
+
+    total[...] = sums[...]
+
+
+def reduce_space(local):
+    flat = local.reshape(CHUNKS, 16, 128)
+    summed = pl.pallas_call(
+        reduce_kernel,
+        out_shape=jax.ShapeDtypeStruct(flat.shape, jnp.float32),
+        in_specs=[pl.BlockSpec(memory_space=pltpu.VMEM)],
+        out_specs=pl.BlockSpec(memory_space=pltpu.VMEM),
+        scratch_shapes=[
+            pltpu.VMEM((PLANE, 16, 128), jnp.float32),
+            pltpu.VMEM((16, 128), jnp.float32),
+            pltpu.VMEM((16, 128), jnp.float32),
+            pltpu.VMEM((CHUNKS, 16, 128), jnp.float32),
+            pltpu.SemaphoreType.DMA((6,)),
+        ],
+        compiler_params=pltpu.CompilerParams(collective_id=0, has_side_effects=True),
+        name="reduce_space",
+    )(flat)
+    return summed.reshape(local.shape)
 
 
 def on_device(volume, weight_first, weight_deep, cotangent):
@@ -91,7 +189,7 @@
     cot_grid = cotangent.reshape(out_chans, deep_planes, deep_rows, deep_depth).astype(jnp.float32)
     grad_pre = (cot_grid * sigma * (1.0 + pre_deep * (1.0 - sigma))).astype(jnp.bfloat16)
     local_grad = weight_terms(grad_pre, deep_in, deep_planes, deep_rows, deep_depth)
-    grad_deep = lax.psum(local_grad, "space")
+    grad_deep = reduce_space(local_grad)
     return (deep_out, grad_deep)
 
 

time: 1870 us -> 251 us (0.13)
  waiting for transfers between devices: 1700 us -> 8.4 us
  Pallas kernels: 0 us -> 85.7 us
    psum x1 -> x0, waiting for transfers between devices: 1690 us -> none  [on_device(): grad_deep = lax.psum(local_grad, 'space')]
    pallas_call x0 -> x1, Pallas kernels: none -> 85.7 us  [reduce_space(): pl.pallas_call(reduce_kernel, out_shape=jax.ShapeDtypeStruct(flat.shape,...]
  transfers between devices with their start and end apart: 7 -> 6, of which waited for: 4 -> 3; matrix products, arithmetic and copies ran while one was open for 0% -> 1% of each run, Pallas kernels for 0% -> 0%
where the time goes in v1:
time: 251 us
  blocking collectives  95.8 us (38%)
  Pallas kernels  85.7 us (34%)
  starting transfers between devices  32.9 us (13%)
  matrix products  20.4 us (8%)
  waiting for transfers between devices  8.4 us (3%)
  local copies, waits for them, and re-layouts  5.49 us (2%)
    all_gather x1, blocking collectives, on_device(): whole = lax.all_gather(pooled, 'chan', axis=2, tiled=True)  95.8 us
    pallas_call x1, Pallas kernels, reduce_space(): pl.pallas_call(reduce_kernel, out_shape=jax.ShapeDtypeStruct(flat.shape,...  85.7 us
    ppermute x3, starting transfers between devices, padded_2(): before = lax.ppermute(last, axis, up)  17 us
    ppermute x3, starting transfers between devices, padded_2(): after = lax.ppermute(leading, axis, down)  16 us
    dot_general x54, matrix products, convolve(): jnp.einsum('oc,cxyz->oxyz', weight[offset_x, offset_y, offset_z], window,...  13.9 us
    ppermute x3, waiting for transfers between devices, padded_2(): after = lax.ppermute(leading, axis, down)  7.18 us
    dot_general x27, matrix products, weight_terms(): jnp.einsum('oxyz,cxyz->oc', grad_pre, window, preferred_element_type=jnp....  6.53 us
  transfers between devices with their start and end apart: 6, of which 3 were waited for; matrix products, arithmetic and copies ran while one was open for 1% of the time, Pallas kernels for 0%

profile of v1, /device:TPU:1, one launch (start us, length us, event | category | flops | bytes accessed | tf_op | source)
XLA Modules:
  0.0 250.6 jit_solution(540745284729479982)
XLA Ops:
  0.6 0.8 copy.25
  1.5 4.6 %collective-permute-start = (bf16[32,1,2,128]{3,0,2,1:T(8,128)(2,1)S(1)}, bf16[32,1,2,128]{3,0,2,1:T(8,128)(2,1)S(1)}, u32[]{:S(2)}, u32[]{:S(2)}) collective-permute-start(bf16[32,1,2,128]{3,0,2,1:T(8,128)(2,1)S(1)} %get-tuple-element.7), channel_id=1, source_target_pairs={{0,16},{16,32},{32,48},{48,64},{64,80},{80,96},{96,112},{112,128},... | collective-permute-start | bytes 49160 | tf_op jit(solution)/shard_map/ppermute | solution.py:16
  6.1 12.8 %collective-permute-start.1 = (bf16[32,1,2,128]{3,0,2,1:T(8,128)(2,1)S(1)}, bf16[32,1,2,128]{3,0,2,1:T(8,128)(2,1)S(1)}, u32[]{:S(2)}, u32[]{:S(2)}) collective-permute-start(bf16[32,1,2,128]{3,0,2,1:T(8,128)(2,1)S(1)} %get-tuple-element.6), channel_id=1, source_target_pairs={{16,0},{32,16},{48,32},{64,48},{80,64},{96,80},{112,96},{128,112},... | collective-permute-start | bytes 49160 | tf_op jit(solution)/shard_map/ppermute | solution.py:17
  18.8 1.0 fusion.124
  19.8 0.8 constant_dynamic-update-slice_fusion.1
  20.6 1.3 collective-permute-start.2
  21.9 1.3 collective-permute-start.3
  23.2 0.9 convolution_bitcast_fusion.11
  24.1 2.8 %collective-permute-done.3 = bf16[32,4,1,128]{3,0,2,1:T(8,128)(2,1)S(1)} collective-permute-done((bf16[32,4,1,128]{3,0,2,1:T(8,128)(2,1)S(1)}, bf16[32,4,1,128]{3,0,2,1:T(8,128)(2,1)S(1)}, u32[]{:S(2)}, u32[]{:S(2)}) %collective-permute-start.3) | collective-permute-done | bytes 32800 | tf_op jit(solution)/shard_map/ppermute | solution.py:17
  32.3 0.3 multiply_reduce_fusion
  32.9 95.8 %all-gather = bf16[64,1024]{0,1:T(8,128)(2,1)S(1)} all-gather(bf16[64,64]{0,1:T(8,128)(2,1)S(1)} %multiply_convert_fusion.1), channel_id=2, replica_groups=mesh['space'=64,'chan'=16] {'chan'}, dimensions={1}, use_global_device_ids=true | all-gather | bytes 139264 | tf_op jit(solution)/shard_map/all_gather | solution.py:175
  128.9 11.1 %collective-permute-start.4 = (bf16[64,1,16,64]{3,0,2,1:T(8,128)(2,1)S(1)}, bf16[64,1,16,64]{3,0,2,1:T(8,128)(2,1)S(1)}, u32[]{:S(2)}, u32[]{:S(2)}) collective-permute-start(bf16[64,1,16,64]{3,0,2,1:T(8,128)(2,1)S(1)} %copy.33), channel_id=1, source_target_pairs={{0,16},{16,32},{32,48},{48,64},{64,80},{80,96},{96,112},{112,128},... | collective-permute-start | bytes 393224 | tf_op jit(solution)/shard_map/ppermute | solution.py:16
  140.0 1.9 collective-permute-start.5
  142.1 1.2 collective-permute-done.4
  143.3 4.4 %collective-permute-done.5 = bf16[64,1,16,64]{3,0,2,1:T(8,128)(2,1)S(1)} collective-permute-done((bf16[64,1,16,64]{3,0,2,1:T(8,128)(2,1)S(1)}, bf16[64,1,16,64]{3,0,2,1:T(8,128)(2,1)S(1)}, u32[]{:S(2)}, u32[]{:S(2)}) %collective-permute-start.5) | collective-permute-done | bytes 131104 | tf_op jit(solution)/shard_map/ppermute | solution.py:17
  147.7 0.4 select_maximum_fusion
  148.3 0.3 fusion.52
  149.0 0.3 convolution_bitcast_fusion.3
  149.3 0.3 convolution_add_fusion.14
  149.6 0.3 convolution_add_fusion.13
  150.4 0.3 convolution_add_fusion.9
  150.6 0.3 convolution_add_fusion.8
  151.4 0.3 convolution_add_fusion.5
  151.8 0.3 convolution_add_fusion.3
  152.2 0.3 convolution_add_fusion.2
  152.6 0.3 fusion.5
  152.9 0.3 fusion.14
  153.2 0.3 fusion.13
  154.3 0.4 fusion.50
  154.9 0.3 convolution_bitcast_fusion.44
  155.3 0.3 convolution_bitcast_fusion.48
  155.6 0.3 convolution_bitcast_fusion.47
  156.1 0.3 convolution_bitcast_fusion.42
  156.4 0.3 convolution_bitcast_fusion.41
  157.1 0.3 convolution_bitcast_fusion.35
  157.6 0.3 convolution_bitcast_fusion.39
  157.8 0.3 convolution_bitcast_fusion.38
  158.3 0.3 convolution_bitcast_fusion.33
  158.6 0.3 convolution_bitcast_fusion.32
  159.1 0.3 convolution_bitcast_fusion.26
  159.5 0.3 convolution_bitcast_fusion.30
  159.8 0.3 convolution_bitcast_fusion.29
  160.3 0.3 convolution_bitcast_fusion.24
  160.6 0.3 convolution_bitcast_fusion.23
  161.5 0.8 reshape.292.terms
  162.3 85.7 %reduce_space.1 = f32[27,16,128]{2,1,0:T(8,128)} custom-call(f32[27,16,128]{2,1,0:T(8,128)} %reshape.292.terms), custom_call_target="tpu_custom_call" | custom-call | tf_op jit(solution)/shard_map/reduce_space/pallas_call | solution.py:149
  248.0 1.8 reshape.293
  249.9 0.8 reshape.291
  (80 shorter events, 11.2 us)
Async XLA Ops:
  0.6 26.4 %copy-start = (bf16[3,3,3,64,32]{3,4,2,1,0:T(8,128)(2,1)S(1)}, bf16[3,3,3,64,32]{3,4,2,1,0:T(8,128)(2,1)}, u32[]{:S(2)}) copy-start(bf16[3,3,3,64,32]{3,4,2,1,0:T(8,128)(2,1)} %param.5) | copy-start | bytes 331780
  1.5 18.3 %collective-permute-start = (bf16[32,1,2,128]{3,0,2,1:T(8,128)(2,1)S(1)}, bf16[32,1,2,128]{3,0,2,1:T(8,128)(2,1)S(1)}, u32[]{:S(2)}, u32[]{:S(2)}) collective-permute-start(bf16[32,1,2,128]{3,0,2,1:T(8,128)(2,1)S(1)} %get-tuple-element.7), channel_id=1, source_target_pairs={{0,16},{16,32},{32,48},{48,64},{64,80},{80,96},{96,112},{112,128},... | collective-permute-start | bytes 49160 | tf_op jit(solution)/shard_map/ppermute | solution.py:16
  6.1 14.5 %collective-permute-start.1 = (bf16[32,1,2,128]{3,0,2,1:T(8,128)(2,1)S(1)}, bf16[32,1,2,128]{3,0,2,1:T(8,128)(2,1)S(1)}, u32[]{:S(2)}, u32[]{:S(2)}) collective-permute-start(bf16[32,1,2,128]{3,0,2,1:T(8,128)(2,1)S(1)} %get-tuple-element.6), channel_id=1, source_target_pairs={{16,0},{32,16},{48,32},{64,48},{80,64},{96,80},{112,96},{128,112},... | collective-permute-start | bytes 49160 | tf_op jit(solution)/shard_map/ppermute | solution.py:17
  20.6 3.5 %collective-permute-start.2 = (bf16[32,4,1,128]{3,0,2,1:T(8,128)(2,1)S(1)}, bf16[32,4,1,128]{3,0,2,1:T(8,128)(2,1)S(1)}, u32[]{:S(2)}, u32[]{:S(2)}) collective-permute-start(bf16[32,4,1,128]{3,0,2,1:T(8,128)(2,1)S(1)} %get-tuple-element.4), channel_id=1, source_target_pairs={{0,1},{1,2},{2,3},{3,4},{4,5},{5,6},{6,7},{7,8},{8,9},{9,10},{10,1... | collective-permute-start | bytes 98312 | tf_op jit(solution)/shard_map/ppermute | solution.py:16
  21.9 5.0 %collective-permute-start.3 = (bf16[32,4,1,128]{3,0,2,1:T(8,128)(2,1)S(1)}, bf16[32,4,1,128]{3,0,2,1:T(8,128)(2,1)S(1)}, u32[]{:S(2)}, u32[]{:S(2)}) collective-permute-start(bf16[32,4,1,128]{3,0,2,1:T(8,128)(2,1)S(1)} %get-tuple-element.5), channel_id=1, source_target_pairs={{1,0},{2,1},{3,2},{4,3},{5,4},{6,5},{7,6},{8,7},{9,8},{10,9},{11,1... | collective-permute-start | bytes 98312 | tf_op jit(solution)/shard_map/ppermute | solution.py:17
  32.7 109.2 %copy-start.2 = (bf16[32,1,1024]{2,0,1:T(8,128)(2,1)S(1)}, bf16[32,1,1024]{2,0,1:T(8,128)(2,1)}, u32[]{:S(2)}) copy-start(bf16[32,1,1024]{2,0,1:T(8,128)(2,1)} %param.7) | copy-start | bytes 196612
  128.9 14.4 %collective-permute-start.4 = (bf16[64,1,16,64]{3,0,2,1:T(8,128)(2,1)S(1)}, bf16[64,1,16,64]{3,0,2,1:T(8,128)(2,1)S(1)}, u32[]{:S(2)}, u32[]{:S(2)}) collective-permute-start(bf16[64,1,16,64]{3,0,2,1:T(8,128)(2,1)S(1)} %copy.33), channel_id=1, source_target_pairs={{0,16},{16,32},{32,48},{48,64},{64,80},{80,96},{96,112},{112,128},... | collective-permute-start | bytes 393224 | tf_op jit(solution)/shard_map/ppermute | solution.py:16
  140.0 7.7 %collective-permute-start.5 = (bf16[64,1,16,64]{3,0,2,1:T(8,128)(2,1)S(1)}, bf16[64,1,16,64]{3,0,2,1:T(8,128)(2,1)S(1)}, u32[]{:S(2)}, u32[]{:S(2)}) collective-permute-start(bf16[64,1,16,64]{3,0,2,1:T(8,128)(2,1)S(1)} %copy.33), channel_id=1, source_target_pairs={{16,0},{32,16},{48,32},{64,48},{80,64},{96,80},{112,96},{128,112},... | collective-permute-start | bytes 393224 | tf_op jit(solution)/shard_map/ppermute | solution.py:17
  142.0 6.1 %copy-start.1 = (bf16[3,3,3,32,64]{4,3,2,1,0:T(8,128)(2,1)S(1)}, bf16[3,3,3,32,64]{4,3,2,1,0:T(8,128)(2,1)}, u32[]{:S(2)}) copy-start(bf16[3,3,3,32,64]{4,3,2,1,0:T(8,128)(2,1)} %param.6) | copy-start | bytes 331780

commit v2 on v0

v2 whole, which is shorter than its diff:
```python
import jax
import jax.numpy as jnp
from jax import lax
from jax.experimental import pallas as pl
from jax.experimental.pallas import tpu as pltpu
from jax.sharding import PartitionSpec as P

MESH = pl.DeviceIdType.MESH
CHUNKS = 27
PLANE = 32
SPACE = 64
CHAN = 16
CELLS = 1024
SIDES = [(dx, dy) for dx in (-1, 0, 1) for dy in (-1, 0, 1) if (dx, dy) != (0, 0)]
SOURCE = {-1: 1, 0: pl.ds(1, 2), 1: 2}
TARGET = {-1: 3, 0: pl.ds(1, 2), 1: 0}


def place(index, high):
    return (index // 8) * 16 + high * 8 + index % 8


def at(space, chan):
    return {"space": space, "chan": chan}


def sized(ref, sem):
    return pltpu.make_async_copy(ref, ref, sem)


def dot(left, right):
    return jnp.dot(left, right, preferred_element_type=jnp.float32)


def step_kernel(
    vol_in, first_in, deep_in, cot_in, out_ref, grad_ref,
    slab, first, deep, cot, first_mat, deep_mat, windows,
    pooled, grid, products, shifted, terms, parts, mine, far, sums,
    local_sems, halo_send, halo_recv, sems,
):
    space = lax.axis_index("space")
    chan = lax.axis_index("chan")
    core = space % 2
    high = (space // 8) % 2
    here = (space // 16) * 8 + space % 8
    other = place(here, 1 - high)
    rest = chan % 4
    group = chan // 4
    side = space - 1 + 2 * core
    has_side = (side >= 0) & (side < SPACE)
    near, away = 2 * core, 2 - 2 * core

    def peer(step):
        return (here + step) % PLANE

    def exists(dx, dy):
        x, y = space + dx, chan + dy
        return (x >= 0) & (x < SPACE) & (y >= 0) & (y < CHAN)

    barrier = pltpu.get_barrier_semaphore()

    def hello(device):
        pl.semaphore_signal(barrier, inc=1, device_id=device, device_id_type=MESH)

    hello(at(other, chan))
    expected = PLANE + 9 + jnp.where(has_side, 3, 0)
    for dx, dy in SIDES:
        here_too = exists(dx, dy)
        expected = expected + jnp.where(here_too, 1, 0)

        @pl.when(here_too)
        def _():
            hello(at(space + dx, chan + dy))

    for step in range(1, 4):
        across = (group + step) % 4 * 4 + rest
        beside = group * 4 + (rest + step) % 4
        hello(at(space, across))
        hello(at(space, beside))
        hello(at(space + 1 - 2 * core, beside))

        @pl.when(has_side)
        def _():
            hello(at(side, across))

    for step in range(1, PLANE):
        hello(at(place(peer(step), high), chan))

    loads = [
        pltpu.make_async_copy(src, dst, local_sems.at[i])
        for i, (src, dst) in enumerate(
            [
                (vol_in, slab.at[pl.ds(1, 2), pl.ds(1, 2)]),
                (first_in, first),
                (deep_in, deep),
                (cot_in, cot),
            ]
        )
    ]
    for load in loads:
        load.start()

    @pl.when(space == 0)
    def _():
        slab[0] = jnp.zeros_like(slab[0])
        pooled[0] = jnp.zeros_like(pooled[0])

    @pl.when(space == SPACE - 1)
    def _():
        slab[3] = jnp.zeros_like(slab[3])
        pooled[2] = jnp.zeros_like(pooled[2])

    @pl.when(chan == 0)
    def _():
        slab[:, 0] = jnp.zeros_like(slab[:, 0])

    @pl.when(chan == CHAN - 1)
    def _():
        slab[:, 3] = jnp.zeros_like(slab[:, 3])

    for load in loads:
        load.wait()
    for a in range(3):
        for b in range(3):
            for c in range(3):
                first_mat[pl.ds((a * 3 + b) * 32, 32), pl.ds(c * 64, 64)] = first[a, b, c]
                deep_mat[pl.ds((b * 3 + c) * 32, 32), pl.ds(a * 64, 64)] = deep[a, b, c]

    pl.semaphore_wait(barrier, expected)

    def rim(n):
        dx, dy = SIDES[n]
        return pltpu.make_async_remote_copy(
            slab.at[SOURCE[dx], SOURCE[dy]],
            slab.at[TARGET[dx], TARGET[dy]],
            halo_send.at[n],
            halo_recv.at[n],
            device_id=at(space + dx, chan + dy),
            device_id_type=MESH,
        )

    for n, (dx, dy) in enumerate(SIDES):

        @pl.when(exists(dx, dy))
        def _():
            rim(n).start()

    for n, (dx, dy) in enumerate(SIDES):

        @pl.when(exists(-dx, -dy))
        def _():
            ref = slab.at[TARGET[dx], TARGET[dy]]
            sized(ref, halo_recv.at[n]).wait()

    for n, (dx, dy) in enumerate(SIDES):

        @pl.when(exists(dx, dy))
        def _():
            ref = slab.at[SOURCE[dx], SOURCE[dy]]
            sized(ref, halo_send.at[n]).wait()

    for x in range(2):
        for y in range(2):
            for a in range(3):
                for b in range(3):
                    windows[pl.ds((a * 3 + b) * 32, 32), pl.ds((x * 2 + y) * 128, 128)] = slab[
                        x + a, y + b
                    ]
    taps = lax.dot_general(
        first_mat[...], windows[...], (((0,), (0,)), ((), ())), preferred_element_type=jnp.float32
    )
    z = lax.broadcasted_iota(jnp.int32, (64, 512), 1) % 128
    pre = taps[64:128]
    pre = pre + jnp.where(z == 0, 0.0, pltpu.roll(taps[0:64], 1, 1))
    pre = pre + jnp.where(z == 127, 0.0, pltpu.roll(taps[128:192], 511, 1))
    act = pre / (1.0 + jnp.exp(-pre))
    added = act[:, 0:128] + act[:, 128:256] + act[:, 256:384] + act[:, 384:512]
    mean = ((added + pltpu.roll(added, 127, 1)) * 0.125).astype(jnp.bfloat16)
    lane = lax.broadcasted_iota(jnp.int32, (128, 128), 0)
    cell = lax.broadcasted_iota(jnp.int32, (128, 128), 1)
    left = jnp.where(lane == 2 * cell, 1.0, 0.0).astype(jnp.bfloat16)
    right = jnp.where(lane == 2 * cell - 128, 1.0, 0.0).astype(jnp.bfloat16)
    piece = dot(mean[0:32], left) + dot(mean[32:64], right)
    pooled[1, rest, group] = piece.astype(jnp.bfloat16)

    def give(src, dst, send, recv, device):
        pltpu.make_async_remote_copy(
            src, dst, sems.at[send], sems.at[recv], device_id=device, device_id_type=MESH
        ).start()

    own = pooled.at[1, rest, group]

    @pl.when(has_side)
    def _():
        for step in range(4):
            across = (group + step) % 4 * 4 + rest
            give(own, pooled.at[away, rest, group], 0, 2, at(side, across))

    for step in range(1, 4):
        across = (group + step) % 4 * 4 + rest
        give(own, own, 1, 3, at(space, across))
    sized(pooled.at[0, 0, pl.ds(0, 3)], sems.at[3]).wait()
    for step in range(4):
        beside = group * 4 + (rest + step) % 4
        give(
            pooled.at[1, rest], pooled.at[near, rest], 4, 5, at(space + 1 - 2 * core, beside)
        )
        if step:
            give(pooled.at[1, rest], pooled.at[1, rest], 6, 7, at(space, beside))

    @pl.when(has_side)
    def _():
        sized(pooled.at[0, 0], sems.at[2]).wait()
        for step in range(1, 4):
            beside = group * 4 + (rest + step) % 4
            give(pooled.at[near, rest], pooled.at[near, rest], 8, 9, at(space, beside))
        sized(pooled.at[0, pl.ds(0, 3)], sems.at[9]).wait()

    sized(pooled.at[0], sems.at[5]).wait()
    sized(pooled.at[0, pl.ds(0, 3)], sems.at[7]).wait()

    lanes = lax.broadcasted_iota(jnp.int32, (32, 128), 1)
    for a in range(3):
        for pair in range(8):
            rows = [
                pooled[a, row % 4, row // 4].astype(jnp.float32) for row in (2 * pair, 2 * pair + 1)
            ]
            low = jnp.where(lanes < 64, rows[0], pltpu.roll(rows[1], 64, 1))
            top = jnp.where(lanes < 64, pltpu.roll(rows[0], 64, 1), rows[1])
            grid[pl.ds(a * 64, 32), pl.ds(pair * 128, 128)] = low.astype(jnp.bfloat16)
            grid[pl.ds(a * 64 + 32, 32), pl.ds(pair * 128, 128)] = top.astype(jnp.bfloat16)

    products[...] = dot(deep_mat[...], grid[...])
    column = lax.broadcasted_iota(jnp.int32, (32, CELLS), 1)
    depth = column % 64

    def tap(b, c):
        return products[pl.ds((b * 3 + c) * 32, 32), :]

    def line(b):
        return (
            tap(b, 1)
            + jnp.where(depth == 0, 0.0, pltpu.roll(tap(b, 0), 1, 1))
            + jnp.where(depth == 63, 0.0, pltpu.roll(tap(b, 2), CELLS - 1, 1))
        )

    pre = line(1)
    pre = pre + jnp.where(column < 64, 0.0, pltpu.roll(line(0), 64, 1))
    pre = pre + jnp.where(column >= CELLS - 64, 0.0, pltpu.roll(line(2), CELLS - 64, 1))
    sigma = 1.0 / (1.0 + jnp.exp(-pre))
    out_ref[...] = (pre * sigma).astype(jnp.bfloat16)
    grad_pre = cot[...].astype(jnp.float32) * sigma * (1.0 + pre * (1.0 - sigma))
    grad_pre = grad_pre.astype(jnp.bfloat16).astype(jnp.float32)
    for b in range(3):
        for c in range(3):
            keep = grad_pre
            if b == 0:
                keep = jnp.where(column < 64, 0.0, keep)
            if b == 2:
                keep = jnp.where(column >= CELLS - 64, 0.0, keep)
            if c == 0:
                keep = jnp.where(depth == 0, 0.0, keep)
            if c == 2:
                keep = jnp.where(depth == 63, 0.0, keep)
            shift = ((b - 1) * 64 + c - 1) % CELLS
            if shift:
                keep = pltpu.roll(keep, shift, 1)
            shifted[pl.ds((b * 3 + c) * 32, 32), :] = keep.astype(jnp.bfloat16)
    local = lax.dot_general(
        shifted[...], grid[...], (((1,), (1,)), ((), ())), preferred_element_type=jnp.float32
    )
    terms[pl.ds(0, 18)] = local[:, 0:128].reshape(18, 16, 128)
    last = jnp.concatenate([local[0:144, 128:192], local[144:288, 128:192]], axis=1)
    terms[pl.ds(18, 9)] = last.reshape(9, 16, 128)

    owner = here < CHUNKS
    for step in range(1, PLANE):
        to = peer(step)

        @pl.when(to < CHUNKS)
        def _():
            give(terms.at[to], parts.at[here], 10, 11, at(place(to, high), chan))

    @pl.when(owner)
    def _():
        parts[here] = terms[here]
        sized(parts.at[pl.ds(0, PLANE - 1)], sems.at[11]).wait()
        mine[...] = jnp.sum(parts[...], axis=0)
        swap = pltpu.make_async_remote_copy(
            mine, far, sems.at[12], sems.at[13], device_id=at(other, chan), device_id_type=MESH
        )
        swap.start()
        swap.wait()
        sums[here] = mine[...] + far[...]
        for step in range(1, PLANE):
            give(sums.at[here], sums.at[here], 14, 15, at(place(peer(step), high), chan))
        sized(sums.at[pl.ds(0, CHUNKS - 1)], sems.at[15]).wait()
        sized(parts.at[pl.ds(0, PLANE - 1)], sems.at[14]).wait()
        sized(terms.at[pl.ds(0, CHUNKS - 1)], sems.at[10]).wait()

    @pl.when(jnp.logical_not(owner))
    def _():
        sized(sums, sems.at[15]).wait()
        sized(terms, sems.at[10]).wait()

    for block in range(18):
        b, c, half = block // 6, (block // 2) % 3, block % 2
        rows = pl.ds(half * 16, 16)
        both = sums[block]
        grad_ref[0, b, c, rows, :] = both[:, 0:64]
        grad_ref[1, b, c, rows, :] = both[:, 64:128]
        third = sums[18 + block % 9]
        grad_ref[2, b, c, rows, :] = third[:, 0:64] if block < 9 else third[:, 64:128]

    @pl.when(has_side)
    def _():
        sized(pooled.at[0, 0], sems.at[0]).wait()
        sized(pooled.at[0, pl.ds(0, 3)], sems.at[8]).wait()

    sized(pooled.at[0, 0, pl.ds(0, 3)], sems.at[1]).wait()
    sized(pooled.at[0], sems.at[4]).wait()
    sized(pooled.at[0, pl.ds(0, 3)], sems.at[6]).wait()


def on_device(volume, weight_first, weight_deep, cotangent):
    bf16, f32 = jnp.bfloat16, jnp.float32
    deep_out, grad_deep = pl.pallas_call(
        step_kernel,
        out_shape=(
            jax.ShapeDtypeStruct((32, CELLS), bf16),
            jax.ShapeDtypeStruct((3, 3, 3, 32, 64), f32),
        ),
        in_specs=[pl.BlockSpec(memory_space=pl.ANY)] * 4,
        out_specs=(
            pl.BlockSpec(memory_space=pltpu.VMEM),
            pl.BlockSpec(memory_space=pltpu.VMEM),
        ),
        scratch_shapes=[
            pltpu.VMEM((4, 4, 32, 128), bf16),
            pltpu.VMEM((3, 3, 3, 32, 64), bf16),
            pltpu.VMEM((3, 3, 3, 32, 64), bf16),
            pltpu.VMEM((32, CELLS), bf16),
            pltpu.VMEM((288, 192), bf16),
            pltpu.VMEM((288, 192), bf16),
            pltpu.VMEM((288, 512), bf16),
            pltpu.VMEM((3, 4, 4, 32, 128), bf16),
            pltpu.VMEM((192, CELLS), bf16),
            pltpu.VMEM((288, CELLS), f32),
            pltpu.VMEM((288, CELLS), bf16),
            pltpu.VMEM((CHUNKS, 16, 128), f32),
            pltpu.VMEM((PLANE, 16, 128), f32),
            pltpu.VMEM((16, 128), f32),
            pltpu.VMEM((16, 128), f32),
            pltpu.VMEM((CHUNKS, 16, 128), f32),
            pltpu.SemaphoreType.DMA((4,)),
            pltpu.SemaphoreType.DMA((8,)),
            pltpu.SemaphoreType.DMA((8,)),
            pltpu.SemaphoreType.DMA((16,)),
        ],
        compiler_params=pltpu.CompilerParams(
            collective_id=0, has_side_effects=True, vmem_limit_bytes=32 * 2**20
        ),
        name="step",
    )(
        jnp.transpose(volume, (1, 2, 0, 3)),
        jnp.transpose(weight_first, (0, 1, 2, 4, 3)),
        weight_deep,
        cotangent.reshape(32, CELLS),
    )
    return deep_out.reshape(32, 1, CELLS), grad_deep


def solution(mesh):
    return jax.shard_map(
        on_device,
        mesh=mesh,
        in_specs=(
            P(None, "space", "chan", None),
            P(),
            P(None, None, None, "chan", None),
            P("chan", "space", None),
        ),
        out_specs=(P("chan", "space", None), P(None, None, None, "chan", None)),
        check_vma=False,
    )
```

time: 1870 us -> 89.7 us (0.05)
  waiting for transfers between devices: 1700 us -> 0 us
  blocking collectives: 95.8 us -> 0 us
  Pallas kernels: 0 us -> 84.7 us
  starting transfers between devices: 33 us -> 0 us
  matrix products: 20.4 us -> 0 us
    psum x1 -> x0, waiting for transfers between devices: 1690 us -> none  [on_device(): grad_deep = lax.psum(local_grad, 'space')]
    all_gather x1 -> x0, blocking collectives: 95.8 us -> none  [on_device(): whole = lax.all_gather(pooled, 'chan', axis=2, tiled=True)]
    pallas_call x0 -> x1, Pallas kernels: none -> 84.7 us  [on_device(): pl.pallas_call(step_kernel, out_shape=(jax.ShapeDtypeStruct((32, CELLS),...]
    ppermute x6 -> x0, starting transfers between devices: 32.9 us -> none  [the longest x3 17 us: padded_2(): before = lax.ppermute(last, axis, up)]
    dot_general x81 -> x0, matrix products: 20.4 us -> none  [the longest x54 13.9 us: convolve(): jnp.einsum('oc,cxyz->oxyz', weight[offset_x, offset_y, offset_z], window,...]
  transfers between devices with their start and end apart: 7 -> 0, of which waited for: 4 -> 0; matrix products, arithmetic and copies ran while one was open for 0% -> 0% of each run, Pallas kernels for 0% -> 0%
where the time goes in v2:
time: 89.7 us; the launch traced here: 89.4 us
  Pallas kernels  84.7 us (94%)
  local copies, waits for them, and re-layouts  4.1 us (5%)
    pallas_call x1, Pallas kernels, on_device(): pl.pallas_call(step_kernel, out_shape=(jax.ShapeDtypeStruct((32, CELLS),...  84.7 us
    unnamed x9, local copies, waits for them, and re-layouts  4.1 us

profile of v2, /device:TPU:1, one launch (start us, length us, event | category | flops | bytes accessed | tf_op | source)
XLA Modules:
  0.0 89.4 jit_solution(14785224374849476998)
XLA Ops:
  0.6 0.0 copy-start.2
  0.6 0.8 copy.8
  1.4 0.0 copy-done.2
  1.5 0.0 copy-start
  1.5 0.9 %copy-done = bf16[3,3,3,64,32]{3,4,2,1,0:T(8,128)(2,1)S(1)} copy-done((bf16[3,3,3,64,32]{3,4,2,1,0:T(8,128)(2,1)S(1)}, bf16[3,3,3,64,32]{3,4,2,1,0:T(8,128)(2,1)}, u32[]{:S(2)}) %copy-start) | copy-done | bytes 110616
  2.4 0.0 copy-start.1
  2.4 0.9 %copy-done.1 = bf16[3,3,3,32,64]{4,3,2,1,0:T(8,128)(2,1)S(1)} copy-done((bf16[3,3,3,32,64]{4,3,2,1,0:T(8,128)(2,1)S(1)}, bf16[3,3,3,32,64]{4,3,2,1,0:T(8,128)(2,1)}, u32[]{:S(2)}) %copy-start.1) | copy-done | bytes 110616
  3.3 84.7 %step.1 = (bf16[32,1024]{1,0:T(8,128)(2,1)S(1)}, f32[3,3,3,32,64]{4,3,2,1,0:T(8,128)S(1)}) custom-call(bf16[2,2,32,128]{3,2,1,0:T(8,128)(2,1)S(1)} %bitcast.7, bf16[3,3,3,32,64]{4,3,2,1,0:T(8,128)(2,1)S(1)} %bitcast.6, bf16[3,3,3,32,64]{4,3,2,1,0:T(8,128)(2,1)S(1)} %copy-done.1, bf16[32,1024]{1,0:T(8,128)(2,1)S(1)} %bitcast.8), custom_call_target="tpu_custom_call" | custom-call | tf_op jit(solution)/shard_map/step/pallas_call | solution.py:327
  88.1 0.6 copy.11
  88.7 0.8 copy.12
Async XLA Ops:
  0.6 0.8 copy-start.2
  1.5 0.9 %copy-start = (bf16[3,3,3,64,32]{3,4,2,1,0:T(8,128)(2,1)S(1)}, bf16[3,3,3,64,32]{3,4,2,1,0:T(8,128)(2,1)}, u32[]{:S(2)}) copy-start(bf16[3,3,3,64,32]{3,4,2,1,0:T(8,128)(2,1)} %param.5) | copy-start | bytes 331780
  2.4 0.9 %copy-start.1 = (bf16[3,3,3,32,64]{4,3,2,1,0:T(8,128)(2,1)S(1)}, bf16[3,3,3,32,64]{4,3,2,1,0:T(8,128)(2,1)}, u32[]{:S(2)}) copy-start(bf16[3,3,3,32,64]{4,3,2,1,0:T(8,128)(2,1)} %deep_in.1) | copy-start | bytes 331780

commit v3 on v2

--- a/solution.py
+++ b/solution.py
@@ -11,15 +11,15 @@
 SPACE = 64
 CHAN = 16
 CELLS = 1024
+OFFSETS = sorted(
+    [(i, j, k) for i in range(4) for j in range(4) for k in range(2) if (i, j, k) != (0, 0, 0)],
+    key=lambda o: (-min(o[0], 4 - o[0]) - min(o[1], 4 - o[1]), o),
+)
 SIDES = [(dx, dy) for dx in (-1, 0, 1) for dy in (-1, 0, 1) if (dx, dy) != (0, 0)]
 SOURCE = {-1: 1, 0: pl.ds(1, 2), 1: 2}
 TARGET = {-1: 3, 0: pl.ds(1, 2), 1: 0}
 
 
-def place(index, high):
-    return (index // 8) * 16 + high * 8 + index % 8
-
-
 def at(space, chan):
     return {"space": space, "chan": chan}
 
@@ -34,7 +34,7 @@
 
 def step_kernel(
     vol_in, first_in, deep_in, cot_in, out_ref, grad_ref,
-    slab, first, deep, cot, first_mat, deep_mat, windows,
+    slab, relay, first, deep, cot, first_mat, deep_mat, windows,
     pooled, grid, products, shifted, terms, parts, mine, far, sums,
     local_sems, halo_send, halo_recv, sems,
 ):
@@ -42,50 +42,40 @@
     chan = lax.axis_index("chan")
     core = space % 2
     high = (space // 8) % 2
-    here = (space // 16) * 8 + space % 8
-    other = place(here, 1 - high)
+    line, row = space // 16, (space // 2) % 4
+    here = line * 8 + row * 2 + core
+    other = space + 8 - 16 * high
     rest = chan % 4
     group = chan // 4
     side = space - 1 + 2 * core
     has_side = (side >= 0) & (side < SPACE)
     near, away = 2 * core, 2 - 2 * core
 
-    def peer(step):
-        return (here + step) % PLANE
+    lines = [(line + step) % 4 for step in range(4)]
+    rows = [(row + step) % 4 for step in range(4)]
+    cores = [core, 1 - core]
+    peers = [
+        (lines[i] * 16 + high * 8 + rows[j] * 2 + cores[k], lines[i] * 8 + rows[j] * 2 + cores[k])
+        for i, j, k in OFFSETS
+    ]
+    edge = space % 8
+    crossing = has_side & ((edge == 0) | (edge == 7))
+    straight = has_side & (edge != 0) & (edge != 7)
 
     def exists(dx, dy):
         x, y = space + dx, chan + dy
-        return (x >= 0) & (x < SPACE) & (y >= 0) & (y < CHAN)
-
-    barrier = pltpu.get_barrier_semaphore()
-
-    def hello(device):
-        pl.semaphore_signal(barrier, inc=1, device_id=device, device_id_type=MESH)
-
-    hello(at(other, chan))
-    expected = PLANE + 9 + jnp.where(has_side, 3, 0)
-    for dx, dy in SIDES:
-        here_too = exists(dx, dy)
-        expected = expected + jnp.where(here_too, 1, 0)
-
-        @pl.when(here_too)
-        def _():
-            hello(at(space + dx, chan + dy))
-
-    for step in range(1, 4):
-        across = (group + step) % 4 * 4 + rest
-        beside = group * 4 + (rest + step) % 4
-        hello(at(space, across))
-        hello(at(space, beside))
-        hello(at(space + 1 - 2 * core, beside))
-
-        @pl.when(has_side)
-        def _():
-            hello(at(side, across))
-
-    for step in range(1, PLANE):
-        hello(at(place(peer(step), high), chan))
-
+        inside = (x >= 0) & (x < SPACE) & (y >= 0) & (y < CHAN)
+        if dx == 0:
+            return inside
+        return inside & (edge != (7 if dx == 1 else 0))
+
+    def give(src, dst, send, recv, device):
+        pltpu.make_async_remote_copy(
+            src, dst, sems.at[send], sems.at[recv], device_id=device, device_id_type=MESH
+        ).start()
+
+    acrosses = [(group + step) % 4 * 4 + rest for step in range(4)]
+    besides = [group * 4 + (rest + step) % 4 for step in range(4)]
     loads = [
         pltpu.make_async_copy(src, dst, local_sems.at[i])
         for i, (src, dst) in enumerate(
@@ -100,6 +90,43 @@
     for load in loads:
         load.start()
 
+    barrier = pltpu.get_barrier_semaphore()
+
+    def hello(device):
+        pl.semaphore_signal(barrier, inc=1, device_id=device, device_id_type=MESH)
+
+    opposite = (chan + 8) % CHAN
+    expected = PLANE - 1 + 6 + jnp.where(straight, 3, 0)
+    for dy in (0, -1, 1):
+        meets = crossing & (chan + dy >= 0) & (chan + dy < CHAN)
+        met = crossing & (opposite + dy >= 0) & (opposite + dy < CHAN)
+        expected = expected + jnp.where(met, 1, 0)
+
+        @pl.when(meets)
+        def _():
+            hello(at(side, (chan + dy + 8) % CHAN))
+
+    for dx, dy in SIDES:
+        here_too = exists(dx, dy)
+        expected = expected + jnp.where(here_too, 1, 0)
+
+        @pl.when(here_too)
+        def _():
+            hello(at(space + dx, chan + dy))
+
+    for across in acrosses[1:]:
+        hello(at(space, across))
+    for beside in besides[1:]:
+        hello(at(space, beside))
+
+    @pl.when(straight)
+    def _():
+        for across in acrosses[1:]:
+            hello(at(side, across))
+
+    for device, _ in peers:
+        hello(at(device, chan))
+
     @pl.when(space == 0)
     def _():
         slab[0] = jnp.zeros_like(slab[0])
@@ -118,14 +145,7 @@
     def _():
         slab[:, 3] = jnp.zeros_like(slab[:, 3])
 
-    for load in loads:
-        load.wait()
-    for a in range(3):
-        for b in range(3):
-            for c in range(3):
-                first_mat[pl.ds((a * 3 + b) * 32, 32), pl.ds(c * 64, 64)] = first[a, b, c]
-                deep_mat[pl.ds((b * 3 + c) * 32, 32), pl.ds(a * 64, 64)] = deep[a, b, c]
-
+    loads[0].wait()
     pl.semaphore_wait(barrier, expected)
 
     def rim(n):
@@ -145,6 +165,21 @@
         def _():
             rim(n).start()
 
+    ahead, behind = 1 + core, 3 * core
+    face = slab.at[ahead, pl.ds(1, 2)]
+
+    @pl.when(crossing)
+    def _():
+        give(face, relay, 19, 20, at(space, opposite))
+
+    for load in loads[1:]:
+        load.wait()
+    for a in range(3):
+        for b in range(3):
+            for c in range(3):
+                first_mat[pl.ds((a * 3 + b) * 32, 32), pl.ds(c * 64, 64)] = first[a, b, c]
+                deep_mat[pl.ds((b * 3 + c) * 32, 32), pl.ds(a * 64, 64)] = deep[a, b, c]
+
     for n, (dx, dy) in enumerate(SIDES):
 
         @pl.when(exists(-dx, -dy))
@@ -158,6 +193,29 @@
         def _():
             ref = slab.at[SOURCE[dx], SOURCE[dy]]
             sized(ref, halo_send.at[n]).wait()
+
+    @pl.when(crossing)
+    def _():
+        sized(relay, sems.at[20]).wait()
+        give(relay, slab.at[3 - behind, pl.ds(1, 2)], 21, 22, at(side, opposite))
+
+        @pl.when(opposite > 0)
+        def _():
+            give(relay.at[0], slab.at[3 - behind, 3], 23, 24, at(side, opposite - 1))
+
+        @pl.when(opposite < CHAN - 1)
+        def _():
+            give(relay.at[1], slab.at[3 - behind, 0], 25, 26, at(side, opposite + 1))
+
+        sized(relay, sems.at[22]).wait()
+
+        @pl.when(chan < CHAN - 1)
+        def _():
+            sized(relay.at[0], sems.at[24]).wait()
+
+        @pl.when(chan > 0)
+        def _():
+            sized(relay.at[0], sems.at[26]).wait()
 
     for x in range(2):
         for y in range(2):
@@ -183,41 +241,38 @@
     piece = dot(mean[0:32], left) + dot(mean[32:64], right)
     pooled[1, rest, group] = piece.astype(jnp.bfloat16)
 
-    def give(src, dst, send, recv, device):
-        pltpu.make_async_remote_copy(
-            src, dst, sems.at[send], sems.at[recv], device_id=device, device_id_type=MESH
-        ).start()
-
     own = pooled.at[1, rest, group]
 
+    for across in acrosses[1:]:
+        give(own, own, 1, 3, at(space, across))
+
     @pl.when(has_side)
     def _():
-        for step in range(4):
-            across = (group + step) % 4 * 4 + rest
+        for across in acrosses:
             give(own, pooled.at[away, rest, group], 0, 2, at(side, across))
 
-    for step in range(1, 4):
-        across = (group + step) % 4 * 4 + rest
-        give(own, own, 1, 3, at(space, across))
+    sibling = at(space + 1 - 2 * core, chan)
     sized(pooled.at[0, 0, pl.ds(0, 3)], sems.at[3]).wait()
-    for step in range(4):
-        beside = group * 4 + (rest + step) % 4
-        give(
-            pooled.at[1, rest], pooled.at[near, rest], 4, 5, at(space + 1 - 2 * core, beside)
-        )
-        if step:
-            give(pooled.at[1, rest], pooled.at[1, rest], 6, 7, at(space, beside))
+    for step in (3, 2, 1):
+        give(pooled.at[1, rest], pooled.at[1, rest], 6, 15 + step, at(space, besides[step]))
+    give(pooled.at[1, rest], pooled.at[near, rest], 4, 5, sibling)
 
     @pl.when(has_side)
     def _():
         sized(pooled.at[0, 0], sems.at[2]).wait()
-        for step in range(1, 4):
-            beside = group * 4 + (rest + step) % 4
-            give(pooled.at[near, rest], pooled.at[near, rest], 8, 9, at(space, beside))
+        for step in (3, 2, 1):
+            give(pooled.at[near, rest], pooled.at[near, rest], 8, 9, at(space, besides[step]))
+
+    for step in (1, 2, 3):
+        sized(pooled.at[0, 0], sems.at[15 + step]).wait()
+        block = (rest + 4 - step) % 4
+        give(pooled.at[1, block], pooled.at[near, block], 4, 5, sibling)
+
+    @pl.when(has_side)
+    def _():
         sized(pooled.at[0, pl.ds(0, 3)], sems.at[9]).wait()
 
     sized(pooled.at[0], sems.at[5]).wait()
-    sized(pooled.at[0, pl.ds(0, 3)], sems.at[7]).wait()
 
     lanes = lax.broadcasted_iota(jnp.int32, (32, 128), 1)
     for a in range(3):
@@ -274,12 +329,11 @@
     terms[pl.ds(18, 9)] = last.reshape(9, 16, 128)
 
     owner = here < CHUNKS
-    for step in range(1, PLANE):
-        to = peer(step)
+    for device, to in peers:
 
         @pl.when(to < CHUNKS)
         def _():
-            give(terms.at[to], parts.at[here], 10, 11, at(place(to, high), chan))
+            give(terms.at[to], parts.at[here], 10, 11, at(device, chan))
 
     @pl.when(owner)
     def _():
@@ -291,26 +345,39 @@
         )
         swap.start()
         swap.wait()
-        sums[here] = mine[...] + far[...]
-        for step in range(1, PLANE):
-            give(sums.at[here], sums.at[here], 14, 15, at(place(peer(step), high), chan))
+        sums[here] = (mine[...] + far[...]).astype(jnp.bfloat16)
+        for device, _ in peers:
+            give(sums.at[here], sums.at[here], 14, 15, at(device, chan))
         sized(sums.at[pl.ds(0, CHUNKS - 1)], sems.at[15]).wait()
-        sized(parts.at[pl.ds(0, PLANE - 1)], sems.at[14]).wait()
+        sized(sums.at[pl.ds(0, PLANE - 1)], sems.at[14]).wait()
         sized(terms.at[pl.ds(0, CHUNKS - 1)], sems.at[10]).wait()
 
     @pl.when(jnp.logical_not(owner))
     def _():
-        sized(sums, sems.at[15]).wait()
+        sized(sums.at[pl.ds(0, CHUNKS)], sems.at[15]).wait()
         sized(terms, sems.at[10]).wait()
 
     for block in range(18):
         b, c, half = block // 6, (block // 2) % 3, block % 2
-        rows = pl.ds(half * 16, 16)
-        both = sums[block]
-        grad_ref[0, b, c, rows, :] = both[:, 0:64]
-        grad_ref[1, b, c, rows, :] = both[:, 64:128]
-        third = sums[18 + block % 9]
-        grad_ref[2, b, c, rows, :] = third[:, 0:64] if block < 9 else third[:, 64:128]
+        part = pl.ds(half * 16, 16)
+        both = sums[block].astype(jnp.float32)
+        grad_ref[0, b, c, part, :] = both[:, 0:64]
+        grad_ref[1, b, c, part, :] = both[:, 64:128]
+        third = sums[18 + block % 9].astype(jnp.float32)
+        grad_ref[2, b, c, part, :] = third[:, 0:64] if block < 9 else third[:, 64:128]
+
+    @pl.when(crossing)
+    def _():
+        sized(relay, sems.at[19]).wait()
+        sized(relay, sems.at[21]).wait()
+
+        @pl.when(opposite > 0)
+        def _():
+            sized(relay.at[0], sems.at[23]).wait()
+
+        @pl.when(opposite < CHAN - 1)
+        def _():
+            sized(relay.at[0], sems.at[25]).wait()
 
     @pl.when(has_side)
     def _():
@@ -330,13 +397,15 @@
             jax.ShapeDtypeStruct((32, CELLS), bf16),
             jax.ShapeDtypeStruct((3, 3, 3, 32, 64), f32),
         ),
-        in_specs=[pl.BlockSpec(memory_space=pl.ANY)] * 4,
+        in_specs=[pl.BlockSpec(memory_space=pl.ANY)]
+        + [pl.BlockSpec(memory_space=pltpu.HBM)] * 3,
         out_specs=(
             pl.BlockSpec(memory_space=pltpu.VMEM),
             pl.BlockSpec(memory_space=pltpu.VMEM),
         ),
         scratch_shapes=[
             pltpu.VMEM((4, 4, 32, 128), bf16),
+            pltpu.VMEM((2, 32, 128), bf16),
             pltpu.VMEM((3, 3, 3, 32, 64), bf16),
             pltpu.VMEM((3, 3, 3, 32, 64), bf16),
             pltpu.VMEM((32, CELLS), bf16),
@@ -351,11 +420,11 @@
             pltpu.VMEM((PLANE, 16, 128), f32),
             pltpu.VMEM((16, 128), f32),
             pltpu.VMEM((16, 128), f32),
-            pltpu.VMEM((CHUNKS, 16, 128), f32),
+            pltpu.VMEM((PLANE, 16, 128), bf16),
             pltpu.SemaphoreType.DMA((4,)),
             pltpu.SemaphoreType.DMA((8,)),
             pltpu.SemaphoreType.DMA((8,)),
-            pltpu.SemaphoreType.DMA((16,)),
+            pltpu.SemaphoreType.DMA((27,)),
         ],
         compiler_params=pltpu.CompilerParams(
             collective_id=0, has_side_effects=True, vmem_limit_bytes=32 * 2**20

time: 89.7 us -> 90 us (level)
  no operation moved by 1% of the time
where the time goes in v3:
time: 90 us; the launch traced here: 89.8 us
  Pallas kernels  85 us (94%)
  local copies, waits for them, and re-layouts  4.1 us (5%)
    pallas_call x1, Pallas kernels, on_device(): pl.pallas_call(step_kernel, out_shape=(jax.ShapeDtypeStruct((32, CELLS),...  85 us
    unnamed x9, local copies, waits for them, and re-layouts  4.1 us

profile of v3, /device:TPU:1, one launch (start us, length us, event | category | flops | bytes accessed | tf_op | source)
XLA Modules:
  0.0 89.8 jit_solution(15983873670503186272)
XLA Ops:
  0.6 0.0 copy-start.2
  0.6 0.8 copy.8
  1.4 0.0 copy-done.2
  1.5 0.0 copy-start
  1.5 0.9 %copy-done = bf16[3,3,3,64,32]{3,4,2,1,0:T(8,128)(2,1)S(1)} copy-done((bf16[3,3,3,64,32]{3,4,2,1,0:T(8,128)(2,1)S(1)}, bf16[3,3,3,64,32]{3,4,2,1,0:T(8,128)(2,1)}, u32[]{:S(2)}) %copy-start) | copy-done | bytes 110616
  2.4 0.0 copy-start.1
  2.4 0.9 %copy-done.1 = bf16[3,3,3,32,64]{4,3,2,1,0:T(8,128)(2,1)S(1)} copy-done((bf16[3,3,3,32,64]{4,3,2,1,0:T(8,128)(2,1)S(1)}, bf16[3,3,3,32,64]{4,3,2,1,0:T(8,128)(2,1)}, u32[]{:S(2)}) %copy-start.1) | copy-done | bytes 110616
  3.3 85.0 %step.1 = (bf16[32,1024]{1,0:T(8,128)(2,1)S(1)}, f32[3,3,3,32,64]{4,3,2,1,0:T(8,128)S(1)}) custom-call(bf16[2,2,32,128]{3,2,1,0:T(8,128)(2,1)S(1)} %bitcast.7, bf16[3,3,3,32,64]{4,3,2,1,0:T(8,128)(2,1)S(1)} %bitcast.6, bf16[3,3,3,32,64]{4,3,2,1,0:T(8,128)(2,1)S(1)} %copy-done.1, bf16[32,1024]{1,0:T(8,128)(2,1)S(1)} %bitcast.8), custom_call_target="tpu_custom_call" | custom-call | tf_op jit(solution)/shard_map/step/pallas_call | solution.py:394
  88.4 0.6 copy.11
  89.0 0.8 copy.12
Async XLA Ops:
  0.6 0.8 copy-start.2
  1.5 0.9 %copy-start = (bf16[3,3,3,64,32]{3,4,2,1,0:T(8,128)(2,1)S(1)}, bf16[3,3,3,64,32]{3,4,2,1,0:T(8,128)(2,1)}, u32[]{:S(2)}) copy-start(bf16[3,3,3,64,32]{3,4,2,1,0:T(8,128)(2,1)} %param.5) | copy-start | bytes 331780
  2.4 0.9 %copy-start.1 = (bf16[3,3,3,32,64]{4,3,2,1,0:T(8,128)(2,1)S(1)}, bf16[3,3,3,32,64]{4,3,2,1,0:T(8,128)(2,1)}, u32[]{:S(2)}) copy-start(bf16[3,3,3,32,64]{4,3,2,1,0:T(8,128)(2,1)} %deep_in.1) | copy-start | bytes 331780

commit v4 on v3

--- a/solution.py
+++ b/solution.py
@@ -36,7 +36,7 @@
     vol_in, first_in, deep_in, cot_in, out_ref, grad_ref,
     slab, relay, first, deep, cot, first_mat, deep_mat, windows,
     pooled, grid, products, shifted, terms, parts, mine, far, sums,
-    local_sems, halo_send, halo_recv, sems,
+    local_sems, halo_send, halo_recv, sems, wide, ready, go, plane,
 ):
     space = lax.axis_index("space")
     chan = lax.axis_index("chan")
@@ -74,7 +74,8 @@
             src, dst, sems.at[send], sems.at[recv], device_id=device, device_id_type=MESH
         ).start()
 
-    acrosses = [(group + step) % 4 * 4 + rest for step in range(4)]
+    low = 1 - group // 2
+    spots = [group, low * (1 - group) + (1 - low) * (5 - group), 1 + low, 3 * low]
     besides = [group * 4 + (rest + step) % 4 for step in range(4)]
     loads = [
         pltpu.make_async_copy(src, dst, local_sems.at[i])
@@ -95,16 +96,18 @@
     def hello(device):
         pl.semaphore_signal(barrier, inc=1, device_id=device, device_id_type=MESH)
 
+    helper = ((edge == 2) & (space > 2)) | ((edge == 5) & (space < SPACE - 3))
     opposite = (chan + 8) % CHAN
-    expected = PLANE - 1 + 6 + jnp.where(straight, 3, 0)
+    outer = (group == 0) | (group == 3)
+    expected = 10 + 3
     for dy in (0, -1, 1):
         meets = crossing & (chan + dy >= 0) & (chan + dy < CHAN)
-        met = crossing & (opposite + dy >= 0) & (opposite + dy < CHAN)
+        met = helper & (opposite + dy >= 0) & (opposite + dy < CHAN)
         expected = expected + jnp.where(met, 1, 0)
 
         @pl.when(meets)
         def _():
-            hello(at(side, (chan + dy + 8) % CHAN))
+            hello(at(side - 2 + 4 * core, (chan + dy + 8) % CHAN))
 
     for dx, dy in SIDES:
         here_too = exists(dx, dy)
@@ -114,18 +117,28 @@
         def _():
             hello(at(space + dx, chan + dy))
 
-    for across in acrosses[1:]:
-        hello(at(space, across))
+    for n in range(3):
+        close = n < 2 or jnp.logical_not(outer)
+        expected = expected + jnp.where(close, 1, 0) + jnp.where(straight & close, 1, 0)
+
+        @pl.when(close)
+        def _():
+            hello(at(space, spots[n + 1] * 4 + rest))
+
+        @pl.when(straight & close)
+        def _():
+            hello(at(side, spots[n + 1] * 4 + rest))
+
     for beside in besides[1:]:
         hello(at(space, beside))
 
-    @pl.when(straight)
-    def _():
-        for across in acrosses[1:]:
-            hello(at(side, across))
-
-    for device, _ in peers:
-        hello(at(device, chan))
+    column = [at(line * 16 + high * 8 + rows[j] * 2 + core, chan) for j in range(1, 4)]
+    hello(at(space + 1 - 2 * core, chan))
+    for i in range(1, 4):
+        for k in range(2):
+            hello(at(lines[i] * 16 + high * 8 + row * 2 + cores[k], chan))
+    for device in column:
+        hello(device)
 
     @pl.when(space == 0)
     def _():
@@ -147,6 +160,15 @@
 
     loads[0].wait()
     pl.semaphore_wait(barrier, expected)
+    pl.semaphore_signal(ready, inc=1, device_id=at(space, opposite), device_id_type=MESH)
+
+    for device in column:
+        pl.semaphore_signal(plane, inc=1, device_id=device, device_id_type=MESH)
+
+    @pl.when(helper)
+    def _():
+        relayed = at(space - 2 + 4 * core, chan)
+        pl.semaphore_signal(go, inc=1, device_id=relayed, device_id_type=MESH)
 
     def rim(n):
         dx, dy = SIDES[n]
@@ -197,6 +219,7 @@
     @pl.when(crossing)
     def _():
         sized(relay, sems.at[20]).wait()
+        pl.semaphore_wait(go, 1)
         give(relay, slab.at[3 - behind, pl.ds(1, 2)], 21, 22, at(side, opposite))
 
         @pl.when(opposite > 0)
@@ -242,31 +265,53 @@
     pooled[1, rest, group] = piece.astype(jnp.bfloat16)
 
     own = pooled.at[1, rest, group]
-
-    for across in acrosses[1:]:
-        give(own, own, 1, 3, at(space, across))
+    sibling = at(space + 1 - 2 * core, chan)
+    flip = jnp.where(crossing, 1, 0)
+    turns = [spots[n] + flip * (spots[3 - n] - spots[n]) for n in range(4)]
+
+    def to_mates(plane, index, send, recv):
+        for step in (3, 2, 1):
+            piece = pooled.at[plane, rest, index]
+            give(piece, piece, send, recv, at(space, besides[step]))
+
+    def own_row(n):
+        if n:
+            sized(own, wide.at[spots[n]]).wait()
+        to_mates(1, spots[n], 6, 27 + n)
+
+    def side_row(n):
+        @pl.when(has_side)
+        def _():
+            sized(own, wide.at[4 + turns[n]]).wait()
+            to_mates(near, turns[n], 8, 9)
+
+    def to_sibling(n):
+        sized(pooled.at[0, 0, pl.ds(0, 3)], sems.at[27 + n]).wait()
+        give(pooled.at[1, :, spots[n]], pooled.at[near, :, spots[n]], 4, 5, sibling)
+
+    pl.semaphore_wait(ready, 1)
+    pl.semaphore_wait(plane, 3)
+    for n in (3, 2, 1):
+        pltpu.make_async_remote_copy(
+            own, own, sems.at[1], wide.at[group],
+            device_id=at(space, spots[n] * 4 + rest), device_id_type=MESH,
+        ).start()
 
     @pl.when(has_side)
     def _():
-        for across in acrosses:
-            give(own, pooled.at[away, rest, group], 0, 2, at(side, across))
-
-    sibling = at(space + 1 - 2 * core, chan)
-    sized(pooled.at[0, 0, pl.ds(0, 3)], sems.at[3]).wait()
-    for step in (3, 2, 1):
-        give(pooled.at[1, rest], pooled.at[1, rest], 6, 15 + step, at(space, besides[step]))
-    give(pooled.at[1, rest], pooled.at[near, rest], 4, 5, sibling)
-
-    @pl.when(has_side)
-    def _():
-        sized(pooled.at[0, 0], sems.at[2]).wait()
-        for step in (3, 2, 1):
-            give(pooled.at[near, rest], pooled.at[near, rest], 8, 9, at(space, besides[step]))
-
-    for step in (1, 2, 3):
-        sized(pooled.at[0, 0], sems.at[15 + step]).wait()
-        block = (rest + 4 - step) % 4
-        give(pooled.at[1, block], pooled.at[near, block], 4, 5, sibling)
+        for n in (3, 2, 1, 0):
+            pltpu.make_async_remote_copy(
+                own, pooled.at[away, rest, group], sems.at[0], wide.at[4 + group],
+                device_id=at(side, spots[n] * 4 + rest), device_id_type=MESH,
+            ).start()
+
+    own_row(0)
+    for n in range(1, 4):
+        side_row(n - 1)
+        own_row(n)
+        to_sibling(n - 1)
+    side_row(3)
+    to_sibling(3)
 
     @pl.when(has_side)
     def _():
@@ -344,10 +389,11 @@
             mine, far, sems.at[12], sems.at[13], device_id=at(other, chan), device_id_type=MESH
         )
         swap.start()
-        swap.wait()
+        swap.wait_recv()
         sums[here] = (mine[...] + far[...]).astype(jnp.bfloat16)
         for device, _ in peers:
             give(sums.at[here], sums.at[here], 14, 15, at(device, chan))
+        swap.wait_send()
         sized(sums.at[pl.ds(0, CHUNKS - 1)], sems.at[15]).wait()
         sized(sums.at[pl.ds(0, PLANE - 1)], sems.at[14]).wait()
         sized(terms.at[pl.ds(0, CHUNKS - 1)], sems.at[10]).wait()
@@ -424,7 +470,11 @@
             pltpu.SemaphoreType.DMA((4,)),
             pltpu.SemaphoreType.DMA((8,)),
             pltpu.SemaphoreType.DMA((8,)),
-            pltpu.SemaphoreType.DMA((27,)),
+            pltpu.SemaphoreType.DMA((31,)),
+            pltpu.SemaphoreType.DMA((8,)),
+            pltpu.SemaphoreType.REGULAR,
+            pltpu.SemaphoreType.REGULAR,
+            pltpu.SemaphoreType.REGULAR,
         ],
         compiler_params=pltpu.CompilerParams(
             collective_id=0, has_side_effects=True, vmem_limit_bytes=32 * 2**20

time: 90 us -> 87.9 us (0.977)
  Pallas kernels: 85 us -> 83 us
    pallas_call x1, Pallas kernels: 85 us -> 83 us  [on_device(): pl.pallas_call(step_kernel, out_shape=(jax.ShapeDtypeStruct((32, CELLS),...]
where the time goes in v4:
time: 87.9 us; the launch traced here: 87.7 us
  Pallas kernels  83 us (94%)
  local copies, waits for them, and re-layouts  4.1 us (5%)
    pallas_call x1, Pallas kernels, on_device(): pl.pallas_call(step_kernel, out_shape=(jax.ShapeDtypeStruct((32, CELLS),...  83 us
    unnamed x9, local copies, waits for them, and re-layouts  4.1 us

profile of v4, /device:TPU:1, one launch (start us, length us, event | category | flops | bytes accessed | tf_op | source)
XLA Modules:
  0.0 87.7 jit_solution(8424544768403683544)
XLA Ops:
  0.6 0.0 copy-start.2
  0.6 0.8 copy.8
  1.4 0.0 copy-done.2
  1.5 0.0 copy-start
  1.5 0.9 %copy-done = bf16[3,3,3,64,32]{3,4,2,1,0:T(8,128)(2,1)S(1)} copy-done((bf16[3,3,3,64,32]{3,4,2,1,0:T(8,128)(2,1)S(1)}, bf16[3,3,3,64,32]{3,4,2,1,0:T(8,128)(2,1)}, u32[]{:S(2)}) %copy-start) | copy-done | bytes 110616
  2.4 0.0 copy-start.1
  2.4 0.9 %copy-done.1 = bf16[3,3,3,32,64]{4,3,2,1,0:T(8,128)(2,1)S(1)} copy-done((bf16[3,3,3,32,64]{4,3,2,1,0:T(8,128)(2,1)S(1)}, bf16[3,3,3,32,64]{4,3,2,1,0:T(8,128)(2,1)}, u32[]{:S(2)}) %copy-start.1) | copy-done | bytes 110616
  3.3 83.0 %step.1 = (bf16[32,1024]{1,0:T(8,128)(2,1)S(1)}, f32[3,3,3,32,64]{4,3,2,1,0:T(8,128)S(1)}) custom-call(bf16[2,2,32,128]{3,2,1,0:T(8,128)(2,1)S(1)} %bitcast.7, bf16[3,3,3,32,64]{4,3,2,1,0:T(8,128)(2,1)S(1)} %bitcast.6, bf16[3,3,3,32,64]{4,3,2,1,0:T(8,128)(2,1)S(1)} %copy-done.1, bf16[32,1024]{1,0:T(8,128)(2,1)S(1)} %bitcast.8), custom_call_target="tpu_custom_call" | custom-call | tf_op jit(solution)/shard_map/step/pallas_call | solution.py:440
  86.3 0.6 copy.11
  86.9 0.8 copy.12
Async XLA Ops:
  0.6 0.8 copy-start.2
  1.5 0.9 %copy-start = (bf16[3,3,3,64,32]{3,4,2,1,0:T(8,128)(2,1)S(1)}, bf16[3,3,3,64,32]{3,4,2,1,0:T(8,128)(2,1)}, u32[]{:S(2)}) copy-start(bf16[3,3,3,64,32]{3,4,2,1,0:T(8,128)(2,1)} %param.5) | copy-start | bytes 331780
  2.4 0.9 %copy-start.1 = (bf16[3,3,3,32,64]{4,3,2,1,0:T(8,128)(2,1)S(1)}, bf16[3,3,3,32,64]{4,3,2,1,0:T(8,128)(2,1)}, u32[]{:S(2)}) copy-start(bf16[3,3,3,32,64]{4,3,2,1,0:T(8,128)(2,1)} %deep_in.1) | copy-start | bytes 331780

commit v5 on v4

--- a/solution.py
+++ b/solution.py
@@ -34,7 +34,7 @@
 
 def step_kernel(
     vol_in, first_in, deep_in, cot_in, out_ref, grad_ref,
-    slab, relay, first, deep, cot, first_mat, deep_mat, windows,
+    slab, vol, relay, first, deep, cot, first_mat, deep_mat, windows,
     pooled, grid, products, shifted, terms, parts, mine, far, sums,
     local_sems, halo_send, halo_recv, sems, wide, ready, go, plane,
 ):
@@ -81,10 +81,10 @@
         pltpu.make_async_copy(src, dst, local_sems.at[i])
         for i, (src, dst) in enumerate(
             [
-                (vol_in, slab.at[pl.ds(1, 2), pl.ds(1, 2)]),
                 (first_in, first),
                 (deep_in, deep),
                 (cot_in, cot),
+                (vol_in, vol),
             ]
         )
     ]
@@ -98,16 +98,20 @@
 
     helper = ((edge == 2) & (space > 2)) | ((edge == 5) & (space < SPACE - 3))
     opposite = (chan + 8) % CHAN
+    helper = helper & (high == 0)
+    by_relay = crossing & (high == 0)
+    direct = crossing & (high == 1)
+    hub = opposite + high * (chan - opposite)
     outer = (group == 0) | (group == 3)
     expected = 10 + 3
     for dy in (0, -1, 1):
         meets = crossing & (chan + dy >= 0) & (chan + dy < CHAN)
-        met = helper & (opposite + dy >= 0) & (opposite + dy < CHAN)
+        met = (helper | direct) & (hub + dy >= 0) & (hub + dy < CHAN)
         expected = expected + jnp.where(met, 1, 0)
 
         @pl.when(meets)
         def _():
-            hello(at(side - 2 + 4 * core, (chan + dy + 8) % CHAN))
+            hello(at(side + high * (4 * core - 2), (chan + dy + 8 * high) % CHAN))
 
     for dx, dy in SIDES:
         here_too = exists(dx, dy)
@@ -158,7 +162,11 @@
     def _():
         slab[:, 3] = jnp.zeros_like(slab[:, 3])
 
-    loads[0].wait()
+    loads[3].wait()
+    block = vol[...].astype(jnp.float32)
+    for x in range(2):
+        for y in range(2):
+            slab[1 + x, 1 + y] = block[:, x, y, :].astype(jnp.bfloat16)
     pl.semaphore_wait(barrier, expected)
     pl.semaphore_signal(ready, inc=1, device_id=at(space, opposite), device_id_type=MESH)
 
@@ -190,11 +198,26 @@
     ahead, behind = 1 + core, 3 * core
     face = slab.at[ahead, pl.ds(1, 2)]
 
-    @pl.when(crossing)
+    def cross(src):
+        give(src, slab.at[3 - behind, pl.ds(1, 2)], 21, 22, at(side, hub))
+
+        @pl.when(hub > 0)
+        def _():
+            give(src.at[0], slab.at[3 - behind, 3], 23, 24, at(side, hub - 1))
+
+        @pl.when(hub < CHAN - 1)
+        def _():
+            give(src.at[1], slab.at[3 - behind, 0], 25, 26, at(side, hub + 1))
+
+    @pl.when(direct)
+    def _():
+        cross(face)
+
+    @pl.when(by_relay)
     def _():
         give(face, relay, 19, 20, at(space, opposite))
 
-    for load in loads[1:]:
+    for load in loads[:3]:
         load.wait()
     for a in range(3):
         for b in range(3):
@@ -209,27 +232,14 @@
             ref = slab.at[TARGET[dx], TARGET[dy]]
             sized(ref, halo_recv.at[n]).wait()
 
-    for n, (dx, dy) in enumerate(SIDES):
-
-        @pl.when(exists(dx, dy))
-        def _():
-            ref = slab.at[SOURCE[dx], SOURCE[dy]]
-            sized(ref, halo_send.at[n]).wait()
-
-    @pl.when(crossing)
+    @pl.when(by_relay)
     def _():
         sized(relay, sems.at[20]).wait()
         pl.semaphore_wait(go, 1)
-        give(relay, slab.at[3 - behind, pl.ds(1, 2)], 21, 22, at(side, opposite))
-
-        @pl.when(opposite > 0)
-        def _():
-            give(relay.at[0], slab.at[3 - behind, 3], 23, 24, at(side, opposite - 1))
-
-        @pl.when(opposite < CHAN - 1)
-        def _():
-            give(relay.at[1], slab.at[3 - behind, 0], 25, 26, at(side, opposite + 1))
-
+        cross(relay)
+
+    @pl.when(crossing)
+    def _():
         sized(relay, sems.at[22]).wait()
 
         @pl.when(chan < CHAN - 1)
@@ -297,30 +307,44 @@
             device_id=at(space, spots[n] * 4 + rest), device_id_type=MESH,
         ).start()
 
+    def to_side(n):
+        pltpu.make_async_remote_copy(
+            own, pooled.at[away, rest, group], sems.at[0], wide.at[4 + group],
+            device_id=at(side, spots[n] * 4 + rest), device_id_type=MESH,
+        ).start()
+
+    later = by_relay & outer
+
+    @pl.when(has_side & jnp.logical_not(later))
+    def _():
+        to_side(3)
+
     @pl.when(has_side)
     def _():
-        for n in (3, 2, 1, 0):
-            pltpu.make_async_remote_copy(
-                own, pooled.at[away, rest, group], sems.at[0], wide.at[4 + group],
-                device_id=at(side, spots[n] * 4 + rest), device_id_type=MESH,
-            ).start()
+        for n in (2, 1, 0):
+            to_side(n)
 
     own_row(0)
-    for n in range(1, 4):
-        side_row(n - 1)
-        own_row(n)
-        to_sibling(n - 1)
+    own_row(1)
+    to_sibling(0)
+    own_row(2)
+
+    @pl.when(later)
+    def _():
+        to_side(3)
+
+    side_row(0)
+    to_sibling(1)
+    side_row(1)
+    own_row(3)
+    to_sibling(2)
+    side_row(2)
     side_row(3)
     to_sibling(3)
 
-    @pl.when(has_side)
-    def _():
-        sized(pooled.at[0, pl.ds(0, 3)], sems.at[9]).wait()
-
-    sized(pooled.at[0], sems.at[5]).wait()
-
     lanes = lax.broadcasted_iota(jnp.int32, (32, 128), 1)
-    for a in range(3):
+
+    def lay_out(a):
         for pair in range(8):
             rows = [
                 pooled[a, row % 4, row // 4].astype(jnp.float32) for row in (2 * pair, 2 * pair + 1)
@@ -330,6 +354,17 @@
             grid[pl.ds(a * 64, 32), pl.ds(pair * 128, 128)] = low.astype(jnp.bfloat16)
             grid[pl.ds(a * 64 + 32, 32), pl.ds(pair * 128, 128)] = top.astype(jnp.bfloat16)
 
+    lay_out(1)
+
+    @pl.when(has_side)
+    def _():
+        sized(pooled.at[0, pl.ds(0, 3)], sems.at[9]).wait()
+
+    sized(pooled.at[0], sems.at[5]).wait()
+
+    lay_out(0)
+    lay_out(2)
+
     products[...] = dot(deep_mat[...], grid[...])
     column = lax.broadcasted_iota(jnp.int32, (32, CELLS), 1)
     depth = column % 64
@@ -348,7 +383,6 @@
     pre = pre + jnp.where(column < 64, 0.0, pltpu.roll(line(0), 64, 1))
     pre = pre + jnp.where(column >= CELLS - 64, 0.0, pltpu.roll(line(2), CELLS - 64, 1))
     sigma = 1.0 / (1.0 + jnp.exp(-pre))
-    out_ref[...] = (pre * sigma).astype(jnp.bfloat16)
     grad_pre = cot[...].astype(jnp.float32) * sigma * (1.0 + pre * (1.0 - sigma))
     grad_pre = grad_pre.astype(jnp.bfloat16).astype(jnp.float32)
     for b in range(3):
@@ -380,6 +414,8 @@
         def _():
             give(terms.at[to], parts.at[here], 10, 11, at(device, chan))
 
+    out_ref[...] = (pre * sigma).astype(jnp.bfloat16)
+
     @pl.when(owner)
     def _():
         parts[here] = terms[here]
@@ -412,16 +448,26 @@
         third = sums[18 + block % 9].astype(jnp.float32)
         grad_ref[2, b, c, part, :] = third[:, 0:64] if block < 9 else third[:, 64:128]
 
+    for n, (dx, dy) in enumerate(SIDES):
+
+        @pl.when(exists(dx, dy))
+        def _():
+            ref = slab.at[SOURCE[dx], SOURCE[dy]]
+            sized(ref, halo_send.at[n]).wait()
+
+    @pl.when(by_relay)
+    def _():
+        sized(relay, sems.at[19]).wait()
+
     @pl.when(crossing)
     def _():
-        sized(relay, sems.at[19]).wait()
         sized(relay, sems.at[21]).wait()
 
-        @pl.when(opposite > 0)
+        @pl.when(hub > 0)
         def _():
             sized(relay.at[0], sems.at[23]).wait()
 
-        @pl.when(opposite < CHAN - 1)
+        @pl.when(hub < CHAN - 1)
         def _():
             sized(relay.at[0], sems.at[25]).wait()
 
@@ -443,7 +489,7 @@
             jax.ShapeDtypeStruct((32, CELLS), bf16),
             jax.ShapeDtypeStruct((3, 3, 3, 32, 64), f32),
         ),
-        in_specs=[pl.BlockSpec(memory_space=pl.ANY)]
+        in_specs=[pl.BlockSpec(memory_space=pltpu.HBM)]
         + [pl.BlockSpec(memory_space=pltpu.HBM)] * 3,
         out_specs=(
             pl.BlockSpec(memory_space=pltpu.VMEM),
@@ -451,6 +497,7 @@
         ),
         scratch_shapes=[
             pltpu.VMEM((4, 4, 32, 128), bf16),
+            pltpu.VMEM((32, 2, 2, 128), bf16),
             pltpu.VMEM((2, 32, 128), bf16),
             pltpu.VMEM((3, 3, 3, 32, 64), bf16),
             pltpu.VMEM((3, 3, 3, 32, 64), bf16),
@@ -477,11 +524,11 @@
             pltpu.SemaphoreType.REGULAR,
         ],
         compiler_params=pltpu.CompilerParams(
-            collective_id=0, has_side_effects=True, vmem_limit_bytes=32 * 2**20
+            collective_id=0, has_side_effects=True, vmem_limit_bytes=55500 * 1024
         ),
         name="step",
     )(
-        jnp.transpose(volume, (1, 2, 0, 3)),
+        volume,
         jnp.transpose(weight_first, (0, 1, 2, 4, 3)),
         weight_deep,
         cotangent.reshape(32, CELLS),

time: 87.9 us -> 87.5 us (level)
    unnamed x9 -> x2, local copies, waits for them, and re-layouts: 4.1 us -> 3.28 us
where the time goes in v5:
time: 87.5 us; the launch traced here: 87.2 us
  Pallas kernels  83.3 us (95%)
  local copies, waits for them, and re-layouts  3.28 us (4%)
    pallas_call x1, Pallas kernels, on_device(): pl.pallas_call(step_kernel, out_shape=(jax.ShapeDtypeStruct((32, CELLS),...  83.3 us
    unnamed x2, local copies, waits for them, and re-layouts  3.28 us

profile of v5, /device:TPU:1, one launch (start us, length us, event | category | flops | bytes accessed | tf_op | source)
XLA Modules:
  0.0 87.2 jit_solution(4600066107728808740)
XLA Ops:
  0.6 83.3 %step.1 = (bf16[32,1024]{1,0:T(8,128)(2,1)}, f32[3,3,3,32,64]{4,3,2,1,0:T(8,128)}) custom-call(bf16[32,2,2,128]{3,2,1,0:T(2,128)(2,1)} %vol_in.1, bf16[3,3,3,32,64]{4,3,2,1,0:T(8,128)(2,1)} %bitcast.3, bf16[3,3,3,32,64]{4,3,2,1,0:T(8,128)(2,1)} %deep_in.1, bf16[32,1024]{1,0:T(8,128)(2,1)} %bitcast.4), custom_call_target="tpu_custom_call" | custom-call | tf_op jit(solution)/shard_map/step/pallas_call | solution.py:486
  84.0 1.5 %copy.8 = bf16[32,1,1024]{2,0,1:T(8,128)(2,1)} copy(bf16[32,1,1024]{2,0,1:T(8,128)(2,1)} %bitcast.5) | data formatting | bytes 131072
  85.4 1.8 %copy.9 = f32[3,3,3,32,64]{4,3,2,1,0:T(8,128)} copy(f32[3,3,3,32,64]{4,3,2,1,0:T(8,128)} %get-tuple-element.9) | data formatting | bytes 442368

commit v6 on v4

--- a/solution.py
+++ b/solution.py
@@ -34,7 +34,7 @@
 
 def step_kernel(
     vol_in, first_in, deep_in, cot_in, out_ref, grad_ref,
-    slab, relay, first, deep, cot, first_mat, deep_mat, windows,
+    slab, vol, relay, first, deep, cot, first_mat, deep_mat, windows,
     pooled, grid, products, shifted, terms, parts, mine, far, sums,
     local_sems, halo_send, halo_recv, sems, wide, ready, go, plane,
 ):
@@ -81,7 +81,7 @@
         pltpu.make_async_copy(src, dst, local_sems.at[i])
         for i, (src, dst) in enumerate(
             [
-                (vol_in, slab.at[pl.ds(1, 2), pl.ds(1, 2)]),
+                (vol_in, vol),
                 (first_in, first),
                 (deep_in, deep),
                 (cot_in, cot),
@@ -159,6 +159,10 @@
         slab[:, 3] = jnp.zeros_like(slab[:, 3])
 
     loads[0].wait()
+    block = vol[...].astype(jnp.float32)
+    for x in range(2):
+        for y in range(2):
+            slab[1 + x, 1 + y] = block[:, x, y, :].astype(jnp.bfloat16)
     pl.semaphore_wait(barrier, expected)
     pl.semaphore_signal(ready, inc=1, device_id=at(space, opposite), device_id_type=MESH)
 
@@ -208,13 +212,6 @@
         def _():
             ref = slab.at[TARGET[dx], TARGET[dy]]
             sized(ref, halo_recv.at[n]).wait()
-
-    for n, (dx, dy) in enumerate(SIDES):
-
-        @pl.when(exists(dx, dy))
-        def _():
-            ref = slab.at[SOURCE[dx], SOURCE[dy]]
-            sized(ref, halo_send.at[n]).wait()
 
     @pl.when(crossing)
     def _():
@@ -313,14 +310,9 @@
     side_row(3)
     to_sibling(3)
 
-    @pl.when(has_side)
-    def _():
-        sized(pooled.at[0, pl.ds(0, 3)], sems.at[9]).wait()
-
-    sized(pooled.at[0], sems.at[5]).wait()
-
     lanes = lax.broadcasted_iota(jnp.int32, (32, 128), 1)
-    for a in range(3):
+
+    def lay_out(a):
         for pair in range(8):
             rows = [
                 pooled[a, row % 4, row // 4].astype(jnp.float32) for row in (2 * pair, 2 * pair + 1)
@@ -330,6 +322,17 @@
             grid[pl.ds(a * 64, 32), pl.ds(pair * 128, 128)] = low.astype(jnp.bfloat16)
             grid[pl.ds(a * 64 + 32, 32), pl.ds(pair * 128, 128)] = top.astype(jnp.bfloat16)
 
+    lay_out(1)
+
+    @pl.when(has_side)
+    def _():
+        sized(pooled.at[0, pl.ds(0, 3)], sems.at[9]).wait()
+
+    sized(pooled.at[0], sems.at[5]).wait()
+
+    lay_out(0)
+    lay_out(2)
+
     products[...] = dot(deep_mat[...], grid[...])
     column = lax.broadcasted_iota(jnp.int32, (32, CELLS), 1)
     depth = column % 64
@@ -348,7 +351,6 @@
     pre = pre + jnp.where(column < 64, 0.0, pltpu.roll(line(0), 64, 1))
     pre = pre + jnp.where(column >= CELLS - 64, 0.0, pltpu.roll(line(2), CELLS - 64, 1))
     sigma = 1.0 / (1.0 + jnp.exp(-pre))
-    out_ref[...] = (pre * sigma).astype(jnp.bfloat16)
     grad_pre = cot[...].astype(jnp.float32) * sigma * (1.0 + pre * (1.0 - sigma))
     grad_pre = grad_pre.astype(jnp.bfloat16).astype(jnp.float32)
     for b in range(3):
@@ -380,6 +382,8 @@
         def _():
             give(terms.at[to], parts.at[here], 10, 11, at(device, chan))
 
+    out_ref[...] = (pre * sigma).astype(jnp.bfloat16)
+
     @pl.when(owner)
     def _():
         parts[here] = terms[here]
@@ -412,6 +416,13 @@
         third = sums[18 + block % 9].astype(jnp.float32)
         grad_ref[2, b, c, part, :] = third[:, 0:64] if block < 9 else third[:, 64:128]
 
+    for n, (dx, dy) in enumerate(SIDES):
+
+        @pl.when(exists(dx, dy))
+        def _():
+            ref = slab.at[SOURCE[dx], SOURCE[dy]]
+            sized(ref, halo_send.at[n]).wait()
+
     @pl.when(crossing)
     def _():
         sized(relay, sems.at[19]).wait()
@@ -443,7 +454,7 @@
             jax.ShapeDtypeStruct((32, CELLS), bf16),
             jax.ShapeDtypeStruct((3, 3, 3, 32, 64), f32),
         ),
-        in_specs=[pl.BlockSpec(memory_space=pl.ANY)]
+        in_specs=[pl.BlockSpec(memory_space=pltpu.HBM)]
         + [pl.BlockSpec(memory_space=pltpu.HBM)] * 3,
         out_specs=(
             pl.BlockSpec(memory_space=pltpu.VMEM),
@@ -451,6 +462,7 @@
         ),
         scratch_shapes=[
             pltpu.VMEM((4, 4, 32, 128), bf16),
+            pltpu.VMEM((32, 2, 2, 128), bf16),
             pltpu.VMEM((2, 32, 128), bf16),
             pltpu.VMEM((3, 3, 3, 32, 64), bf16),
             pltpu.VMEM((3, 3, 3, 32, 64), bf16),
@@ -477,11 +489,11 @@
             pltpu.SemaphoreType.REGULAR,
         ],
         compiler_params=pltpu.CompilerParams(
-            collective_id=0, has_side_effects=True, vmem_limit_bytes=32 * 2**20
+            collective_id=0, has_side_effects=True, vmem_limit_bytes=55500 * 1024
         ),
         name="step",
     )(
-        jnp.transpose(volume, (1, 2, 0, 3)),
+        volume,
         jnp.transpose(weight_first, (0, 1, 2, 4, 3)),
         weight_deep,
         cotangent.reshape(32, CELLS),

time: 87.9 us -> 87.1 us (level)
    unnamed x9 -> x2, local copies, waits for them, and re-layouts: 4.1 us -> 3.28 us
where the time goes in v6:
time: 87.1 us; the launch traced here: 86.9 us
  Pallas kernels  83 us (95%)
  local copies, waits for them, and re-layouts  3.28 us (4%)
    pallas_call x1, Pallas kernels, on_device(): pl.pallas_call(step_kernel, out_shape=(jax.ShapeDtypeStruct((32, CELLS),...  83 us
    unnamed x2, local copies, waits for them, and re-layouts  3.28 us

profile of v6, /device:TPU:1, one launch (start us, length us, event | category | flops | bytes accessed | tf_op | source)
XLA Modules:
  0.0 86.9 jit_solution(15202937231574213725)
XLA Ops:
  0.6 83.0 %step.1 = (bf16[32,1024]{1,0:T(8,128)(2,1)}, f32[3,3,3,32,64]{4,3,2,1,0:T(8,128)}) custom-call(bf16[32,2,2,128]{3,2,1,0:T(2,128)(2,1)} %vol_in.1, bf16[3,3,3,32,64]{4,3,2,1,0:T(8,128)(2,1)} %bitcast.3, bf16[3,3,3,32,64]{4,3,2,1,0:T(8,128)(2,1)} %deep_in.1, bf16[32,1024]{1,0:T(8,128)(2,1)} %bitcast.4), custom_call_target="tpu_custom_call" | custom-call | tf_op jit(solution)/shard_map/step/pallas_call | solution.py:451
  83.6 1.5 %copy.8 = bf16[32,1,1024]{2,0,1:T(8,128)(2,1)} copy(bf16[32,1,1024]{2,0,1:T(8,128)(2,1)} %bitcast.5) | data formatting | bytes 131072
  85.1 1.8 %copy.9 = f32[3,3,3,32,64]{4,3,2,1,0:T(8,128)} copy(f32[3,3,3,32,64]{4,3,2,1,0:T(8,128)} %get-tuple-element.9) | data formatting | bytes 442368
